TPU v7x, 32 devices: a whole 2x2x4 slice. The times are simulated.
32 devices in a mesh: wide: 8 (over z, x), narrow: 4 (over y, core).
Axes of the slice: x: 2, y: 2, z: 4, core: 2. Of those that a mesh axis runs over, the one named last changes fastest.
Arguments:
- embeddings: bfloat16 [16384, 1024], P(('wide', 'narrow')), may hold values from -32 to 32
- valid: int32 [16384], P(('wide', 'narrow')), may hold values from 0 to 1, as said below
Outputs:
- whitened: bfloat16 [16384, 1024], P(('wide', 'narrow'))
Inputs may be any that keep to these rules, and one draw needn't show every extreme that they name: The first row of every aligned block of 16 rows has valid = 1.
All inputs are finite; a program needn't handle non-finite values.
Results may differ from a plain program's by a relative error of at most 0.001.
Values sent between devices are 32-bit elements; how exact they have to be, the bound alone decides.
No kernel may reach another device: no remote copies, remote signals or barrier semaphores. Data moves between devices by JAX's collectives and lax.ppermute only.
A program may use at most 64 MiB of HBM per device.

v0:
```python
import jax
import jax.numpy as jnp
from jax import lax
from jax.sharding import PartitionSpec as P


def shifted_scatter(gram, count_local, sums_local, center):
    return (
        gram
        - sums_local[:, None] * center[None, :]
        - center[:, None] * sums_local[None, :]
        + count_local * center[:, None] * center[None, :]
    )


def narrow_rows(term):
    return lax.psum_scatter(term, "narrow", scatter_dimension=0, tiled=True)


def on_device(embeddings, valid):
    width = embeddings.shape[1]
    narrow_count = lax.axis_size("narrow")
    row_span = width // narrow_count
    offset = lax.axis_index("narrow") * row_span
    mask_half = valid.astype(jnp.bfloat16)
    count_local = jnp.sum(valid.astype(jnp.float32))
    masked = embeddings * mask_half[:, None]
    gram = lax.dot_general(
        masked, embeddings, (((0,), (0,)), ((), ())), preferred_element_type=jnp.float32
    )
    sums_local = jnp.dot(mask_half[None, :], embeddings, preferred_element_type=jnp.float32)[0]
    count, sums = lax.psum((count_local, sums_local), ("wide", "narrow"))
    term = shifted_scatter(gram, count_local, sums_local, sums / count)
    level_rows = narrow_rows(term)
    own_rows = lax.psum(level_rows, "wide")
    center = sums / count
    cov_rows = own_rows / count
    ident_rows = (
        lax.broadcasted_iota(jnp.int32, (row_span, width), 0) + offset
        == lax.broadcasted_iota(jnp.int32, (row_span, width), 1)
    ).astype(jnp.float32)
    diag_block = lax.dynamic_slice_in_dim(cov_rows, offset, row_span, 1)
    trace_part = jnp.sum(jnp.diagonal(diag_block))
    square_part = jnp.sum(cov_rows * cov_rows)
    trace_cov, square_sum = lax.psum((trace_part, square_part), "narrow")
    ridge_add = 0.05 * trace_cov / width + 1e-06
    norm_frob = jnp.sqrt(square_sum + 2.0 * ridge_add * trace_cov + width * ridge_add * ridge_add)
    base_rows = (cov_rows + ridge_add * ident_rows) / norm_frob
    root_rows = (3.0 * ident_rows - base_rows) / 2.0
    root_full = lax.all_gather(root_rows, "narrow", axis=0, tiled=True)
    first = jnp.dot(
        base_rows, root_full, precision=lax.Precision.HIGHEST, preferred_element_type=jnp.float32
    )
    second = jnp.dot(
        first, root_full, precision=lax.Precision.HIGHEST, preferred_element_type=jnp.float32
    )
    factor = (3.0 * ident_rows - second) / 2.0
    root_rows = jnp.dot(
        factor, root_full, precision=lax.Precision.HIGHEST, preferred_element_type=jnp.float32
    )
    centered_x = embeddings.astype(jnp.float32) - center
    product = jnp.dot(
        centered_x,
        lax.all_gather(root_rows, "narrow", axis=0, tiled=True),
        precision=lax.Precision.HIGHEST,
        preferred_element_type=jnp.float32,
    )
    return (product / jnp.sqrt(norm_frob)).astype(jnp.bfloat16)


def solution(mesh):
    in_specs = (P(("wide", "narrow"), None), P(("wide", "narrow")))
    out_specs = P(("wide", "narrow"), None)
    return jax.shard_map(
        on_device, mesh=mesh, in_specs=in_specs, out_specs=out_specs, check_vma=False
    )
```

profile of v0, /device:TPU:0, one launch (start us, length us, event | category | flops | bytes accessed | tf_op | source)
XLA Modules:
  0.0 300.6 jit_solution(4755402428084836865)
XLA Ops:
  6.5 0.0 reduce-scatter.2.cloned.1.call-start
  6.5 0.7 convert_element_type.14
  7.2 1.3 convert_reduce_fusion
  8.5 1.5 fusion.11
  10.0 42.1 %all-reduce = (f32[1024]{0:T(1024)S(1)}, f32[]{:T(128)}) all-reduce(f32[1024]{0:T(1024)S(1)} %bitcast.12, f32[]{:T(128)} %convert_reduce_fusion), channel_id=1, replica_groups=mesh['wide'=8,'narrow'=4] {'wide','narrow'}, use_global_device_ids=true, to_apply=%region_0.0 | all-reduce | flops 1025 | bytes 8200 | tf_op jit(solution)/shard_map/psum | solution.py:32
  52.1 1.3 broadcast_multiply_fusion
  53.4 5.3 %multiply_add_fusion = f32[1024,1024]{1,0:T(8,128)} fusion(bf16[512,1024]{1,0:T(8,128)(2,1)} %param.2, f32[1024]{0:T(1024)S(1)} %get-tuple-element.11, f32[1024]{0:T(1024)S(1)} %bitcast.13, f32[1024]{0:T(1024)S(1)} %get-tuple-element.12, bf16[512]{0:T(512)(128)(2,1)S(1)} %convert_element_type.14), kind=kOutput, calls=%fused_computation.1 | convolution fusion | flops 1080557568 | bytes 5256192 | tf_op jit(solution)/shard_map/dot_general | solution.py:28
  58.7 0.0 reduce-scatter.2.cloned.1.call-update
  58.7 0.0 all-reduce.4.cloned.1.call-start
  58.8 44.7 %reduce-scatter.2.cloned.1.call-done = f32[256,1024]{1,0:T(8,128)} async-done(((f32[1024,1024]{1,0:T(8,128)}), f32[256,1024]{1,0:T(8,128)}) %reduce-scatter.2.cloned.1.call-update) | async-done | bytes 1048592 | tf_op jit(solution)/shard_map/reduce_scatter | solution.py:17
  103.5 0.0 all-reduce.4.cloned.1.call-update
  103.5 0.0 all-gather.3.cloned.1.call-start
  103.6 81.6 %all-reduce.4.cloned.1.call-done = f32[256,1024]{1,0:T(8,128)} async-done(((f32[256,1024]{1,0:T(8,128)}), f32[256,1024]{1,0:T(8,128)}) %all-reduce.4.cloned.1.call-update) | async-done | bytes 1048592 | tf_op jit(solution)/shard_map/psum | solution.py:35
  185.2 2.7 multiply_reduce_fusion
  188.0 2.3 gather_fusion
  190.4 0.7 reduce_sum.28
  191.0 7.2 %all-reduce.1 = (f32[]{:T(128)}, f32[]{:T(128)}) all-reduce(f32[]{:T(128)} %get-tuple-element.9, f32[]{:T(128)} %reduce_sum.28), channel_id=1, replica_groups=mesh['wide'=8,'narrow'=4] {'narrow'}, use_global_device_ids=true, to_apply=%region_8.9 | all-reduce | flops 2 | bytes 16 | tf_op jit(solution)/shard_map/psum | solution.py:45
  200.3 1.3 fusion.7
  201.6 0.0 all-gather.3.cloned.1.call-update
  201.6 0.2 all-gather.5.cloned.1.call-start
  201.8 33.4 %all-gather.3.cloned.1.call-done = f32[1024,1024]{1,0:T(8,128)} async-done(((f32[256,1024]{1,0:T(8,128)}), f32[1024,1024]{1,0:T(8,128)}) %all-gather.3.cloned.1.call-update) | async-done | bytes 4194320 | tf_op jit(solution)/shard_map/all_gather | solution.py:50
  235.2 0.0 copy-start
  235.2 6.1 %fusion.10 = f32[256,1024]{1,0:T(8,128)S(1)} fusion(f32[1024,1024]{1,0:T(8,128)} %all-gather.3.cloned.1.call-done, f32[256,1024]{1,0:T(8,128)S(1)} %get-tuple-element.10, f32[]{:T(128)S(6)} %sqrt.6, f32[]{:T(128)S(6)} %add.45, s32[256]{0:T(256)S(1)} %iota_add_fusion), kind=kOutput, calls=%fused_computation.23 | convolution fusion | flops 3222274048 | bytes 6292488 | tf_op jit(solution)/shard_map/dot_general | solution.py:51
  241.4 0.0 copy-done
  241.4 3.7 %fusion.4 = f32[256,1024]{1,0:T(8,128)S(1)} fusion(f32[256,1024]{1,0:T(8,128)S(1)} %fusion.10, f32[1024,1024]{1,0:T(8,128)S(1)} %copy-done, s32[256]{0:T(256)S(1)} %iota_add_fusion), kind=kOutput, calls=%fused_computation.9 | convolution fusion | flops 3222274048 | bytes 6292480 | tf_op jit(solution)/shard_map/dot_general | solution.py:54
  245.1 0.0 copy-start.1
  245.2 4.7 %fusion.12 = f32[256,1024]{1,0:T(8,128)} fusion(f32[256,1024]{1,0:T(8,128)S(1)} %fusion.4, f32[1024,1024]{1,0:T(8,128)S(1)} %copy-done), kind=kOutput, calls=%fused_computation.25 | convolution fusion | flops 3221225472 | bytes 6291456 | tf_op jit(solution)/shard_map/dot_general | solution.py:58
  249.8 0.0 all-gather.5.cloned.1.call-update
  249.9 34.6 %all-gather.5.cloned.1.call-done = f32[1024,1024]{1,0:T(8,128)} async-done(((f32[256,1024]{1,0:T(8,128)}), f32[1024,1024]{1,0:T(8,128)}) %all-gather.5.cloned.1.call-update) | async-done | bytes 4194320 | tf_op jit(solution)/shard_map/all_gather | solution.py:64
  284.5 0.0 copy-done.1
  284.5 9.6 %divide_convert_fusion = bf16[512,1024]{1,0:T(8,128)(2,1)} fusion(f32[1024,1024]{1,0:T(8,128)} %all-gather.5.cloned.1.call-done, bf16[512,1024]{1,0:T(8,128)(2,1)S(1)} %copy-done.1, f32[]{:T(128)S(6)} %sqrt.7, f32[1024]{0:T(1024)S(1)} %get-tuple-element.12), kind=kOutput, calls=%fused_computation.2 | convolution fusion | flops 6444548096 | bytes 6295556 | tf_op jit(solution)/shard_map/dot_general | solution.py:62
  (4 shorter events, 0.0 us)
Async XLA Ops:
  6.5 97.0 %reduce-scatter.2.cloned.1.call-start = ((), (), s32[]{:S(2)}) async-start(), calls=%async_computation.1 | async-start | bytes 5242880 | tf_op jit(solution)/shard_map/reduce_scatter | solution.py:17
  58.7 126.5 %all-reduce.4.cloned.1.call-start = ((), (), s32[]{:S(2)}) async-start(), calls=%async_computation.2 | async-start | bytes 2097152 | tf_op jit(solution)/shard_map/psum | solution.py:35
  103.5 131.7 %all-gather.3.cloned.1.call-start = ((), (), s32[]{:S(2)}) async-start(), calls=%async_computation.3 | async-start | bytes 5242880 | tf_op jit(solution)/shard_map/all_gather | solution.py:50
  201.6 82.9 %all-gather.5.cloned.1.call-start = ((), (), s32[]{:S(2)}) async-start(), calls=%async_computation.4 | async-start | bytes 5242880 | tf_op jit(solution)/shard_map/all_gather | solution.py:64
  235.2 6.1 %copy-start = (f32[1024,1024]{1,0:T(8,128)S(1)}, f32[1024,1024]{1,0:T(8,128)}, u32[]{:S(2)}) copy-start(f32[1024,1024]{1,0:T(8,128)} %all-gather.3.cloned.1.call-done) | copy-start | bytes 12582916
  245.1 39.3 %copy-start.1 = (bf16[512,1024]{1,0:T(8,128)(2,1)S(1)}, bf16[512,1024]{1,0:T(8,128)(2,1)}, u32[]{:S(2)}) copy-start(bf16[512,1024]{1,0:T(8,128)(2,1)} %param.2) | copy-start | bytes 3145732
Sparse Core Ops, SparseCore 0:
  58.9 44.6 reduce-scatter.1
  107.0 78.1 all-reduce.3
  201.7 33.4 all-gather.2
  250.0 34.4 all-gather.4
where the time goes:
time: 301 us
  waiting for transfers between devices  194 us (64%)
  blocking collectives  49.3 us (16%)
  matrix products  30.9 us (10%)
  between operations  15.3 us (5%)
  other arithmetic  7.97 us (3%)
    psum x1, waiting for transfers between devices, on_device(): own_rows = lax.psum(level_rows, 'wide')  81.6 us
    reduce_scatter x1, waiting for transfers between devices, narrow_rows(): return lax.psum_scatter(term, 'narrow', scatter_dimension=0, tiled=True)  44.7 us
    psum x1, blocking collectives, on_device(): count, sums = lax.psum((count_local, sums_local), ('wide', 'narrow'))  42.1 us
    all_gather x1, waiting for transfers between devices, on_device(): lax.all_gather(root_rows, 'narrow', axis=0, tiled=True)  34.6 us
    all_gather x1, waiting for transfers between devices, on_device(): root_full = lax.all_gather(root_rows, 'narrow', axis=0, tiled=True)  33.4 us
    dot_general x1, matrix products, on_device(): jnp.dot(centered_x, lax.all_gather(root_rows, 'narrow', axis=0, tiled=Tru...  9.62 us
    psum x1, blocking collectives, on_device(): trace_cov, square_sum = lax.psum((trace_part, square_part), 'narrow')  7.19 us
    dot_general x1, matrix products, on_device(): jnp.dot(base_rows, root_full, precision=lax.Precision.HIGHEST, preferred_...  6.13 us
  transfers between devices with their start and end apart: 4, of which 4 were waited for; matrix products, arithmetic and copies ran while one was open for 0% of the time, Pallas kernels for 0%

commit v1 on v0

--- a/solution.py
+++ b/solution.py
@@ -2,6 +2,11 @@
 import jax.numpy as jnp
 from jax import lax
 from jax.sharding import PartitionSpec as P
+
+
+def one_after_other(array, inner_axis, outer_axis):
+    inner = lax.psum(array, inner_axis)
+    return lax.psum(inner, outer_axis)
 
 
 def shifted_scatter(gram, count_local, sums_local, center):
@@ -29,7 +34,7 @@
         masked, embeddings, (((0,), (0,)), ((), ())), preferred_element_type=jnp.float32
     )
     sums_local = jnp.dot(mask_half[None, :], embeddings, preferred_element_type=jnp.float32)[0]
-    count, sums = lax.psum((count_local, sums_local), ("wide", "narrow"))
+    count, sums = one_after_other((count_local, sums_local), "narrow", "wide")
     term = shifted_scatter(gram, count_local, sums_local, sums / count)
     level_rows = narrow_rows(term)
     own_rows = lax.psum(level_rows, "wide")

time: 301 us -> 287 us (0.953)
  blocking collectives: 49.3 us -> 39 us
    psum x1 -> x2, blocking collectives: 42.1 us -> 31.8 us  [the longest x1 22.5 us: one_after_other(): return lax.psum(inner, outer_axis)]
    reduce_scatter x1, waiting for transfers between devices: 44.7 us -> 40.9 us  [narrow_rows(): return lax.psum_scatter(term, 'narrow', scatter_dimension=0, tiled=True)]
where the time goes in v1:
time: 287 us; the launch traced here: 286 us
  waiting for transfers between devices  191 us (67%)
  blocking collectives  39 us (14%)
  matrix products  31 us (11%)
  between operations  15.3 us (5%)
  other arithmetic  7.97 us (3%)
    psum x1, waiting for transfers between devices, on_device(): own_rows = lax.psum(level_rows, 'wide')  81.6 us
    reduce_scatter x1, waiting for transfers between devices, narrow_rows(): return lax.psum_scatter(term, 'narrow', scatter_dimension=0, tiled=True)  40.9 us
    all_gather x1, waiting for transfers between devices, on_device(): lax.all_gather(root_rows, 'narrow', axis=0, tiled=True)  34.6 us
    all_gather x1, waiting for transfers between devices, on_device(): root_full = lax.all_gather(root_rows, 'narrow', axis=0, tiled=True)  33.4 us
    psum x1, blocking collectives, one_after_other(): return lax.psum(inner, outer_axis)  22.5 us
    dot_general x1, matrix products, on_device(): jnp.dot(centered_x, lax.all_gather(root_rows, 'narrow', axis=0, tiled=Tru...  9.62 us
    psum x1, blocking collectives, one_after_other(): inner = lax.psum(array, inner_axis)  9.24 us
    psum x1, blocking collectives, on_device(): trace_cov, square_sum = lax.psum((trace_part, square_part), 'narrow')  7.19 us
  transfers between devices with their start and end apart: 4, of which 4 were waited for; matrix products, arithmetic and copies ran while one was open for 0% of the time, Pallas kernels for 0%

profile of v1, /device:TPU:0, one launch (start us, length us, event | category | flops | bytes accessed | tf_op | source)
XLA Modules:
  0.0 286.4 jit_solution(3160154486537890468)
XLA Ops:
  6.5 0.0 reduce-scatter.2.cloned.1.call-start
  6.5 0.7 convert_element_type.14
  7.2 1.3 convert_reduce_fusion
  8.5 1.5 fusion.11
  10.0 9.2 %all-reduce.2 = (f32[1024]{0:T(1024)S(1)}, f32[]{:T(128)}) all-reduce(f32[1024]{0:T(1024)S(1)} %bitcast.12, f32[]{:T(128)} %convert_reduce_fusion), channel_id=1, replica_groups=mesh['wide'=8,'narrow'=4] {'narrow'}, use_global_device_ids=true, to_apply=%region_0.0 | all-reduce | flops 1025 | bytes 8200 | tf_op jit(solution)/shard_map/psum | solution.py:8
  19.2 22.5 %all-reduce = (f32[1024]{0:T(1024)S(1)}, f32[]{:T(128)}) all-reduce(f32[1024]{0:T(1024)S(1)} %get-tuple-element.9, f32[]{:T(128)} %get-tuple-element.10), channel_id=1, replica_groups=mesh['wide'=8,'narrow'=4] {'wide'}, use_global_device_ids=true, to_apply=%region_1.0 | all-reduce | flops 1025 | bytes 8200 | tf_op jit(solution)/shard_map/psum | solution.py:9
  41.8 1.3 broadcast_multiply_fusion
  43.0 5.3 %multiply_add_fusion = f32[1024,1024]{1,0:T(8,128)} fusion(bf16[512,1024]{1,0:T(8,128)(2,1)} %param.2, f32[1024]{0:T(1024)S(1)} %get-tuple-element.13, f32[1024]{0:T(1024)S(1)} %bitcast.13, f32[1024]{0:T(1024)S(1)} %get-tuple-element.14, bf16[512]{0:T(512)(128)(2,1)S(1)} %convert_element_type.14), kind=kOutput, calls=%fused_computation.1 | convolution fusion | flops 1080557568 | bytes 5256192 | tf_op jit(solution)/shard_map/dot_general | solution.py:33
  48.4 0.0 reduce-scatter.2.cloned.1.call-update
  48.4 0.0 all-reduce.5.cloned.1.call-start
  48.4 40.9 %reduce-scatter.2.cloned.1.call-done = f32[256,1024]{1,0:T(8,128)} async-done(((f32[1024,1024]{1,0:T(8,128)}), f32[256,1024]{1,0:T(8,128)}) %reduce-scatter.2.cloned.1.call-update) | async-done | bytes 1048592 | tf_op jit(solution)/shard_map/reduce_scatter | solution.py:22
  89.4 0.0 all-reduce.5.cloned.1.call-update
  89.4 0.0 all-gather.3.cloned.1.call-start
  89.5 81.6 %all-reduce.5.cloned.1.call-done = f32[256,1024]{1,0:T(8,128)} async-done(((f32[256,1024]{1,0:T(8,128)}), f32[256,1024]{1,0:T(8,128)}) %all-reduce.5.cloned.1.call-update) | async-done | bytes 1048592 | tf_op jit(solution)/shard_map/psum | solution.py:40
  171.0 2.7 multiply_reduce_fusion
  173.8 2.3 gather_fusion
  176.2 0.7 reduce_sum.28
  176.8 7.2 %all-reduce.1 = (f32[]{:T(128)}, f32[]{:T(128)}) all-reduce(f32[]{:T(128)} %get-tuple-element.11, f32[]{:T(128)} %reduce_sum.28), channel_id=1, replica_groups=mesh['wide'=8,'narrow'=4] {'narrow'}, use_global_device_ids=true, to_apply=%region_10.11 | all-reduce | flops 2 | bytes 16 | tf_op jit(solution)/shard_map/psum | solution.py:50
  186.1 1.3 fusion.7
  187.4 0.0 all-gather.3.cloned.1.call-update
  187.4 0.2 all-gather.5.cloned.1.call-start
  187.7 33.4 %all-gather.3.cloned.1.call-done = f32[1024,1024]{1,0:T(8,128)} async-done(((f32[256,1024]{1,0:T(8,128)}), f32[1024,1024]{1,0:T(8,128)}) %all-gather.3.cloned.1.call-update) | async-done | bytes 4194320 | tf_op jit(solution)/shard_map/all_gather | solution.py:55
  221.1 0.0 copy-start
  221.1 6.1 %fusion.10 = f32[256,1024]{1,0:T(8,128)S(1)} fusion(f32[1024,1024]{1,0:T(8,128)} %all-gather.3.cloned.1.call-done, f32[256,1024]{1,0:T(8,128)S(1)} %get-tuple-element.12, f32[]{:T(128)S(6)} %sqrt.6, f32[]{:T(128)S(6)} %add.49, s32[256]{0:T(256)S(1)} %iota_add_fusion), kind=kOutput, calls=%fused_computation.23 | convolution fusion | flops 3222274048 | bytes 6292488 | tf_op jit(solution)/shard_map/dot_general | solution.py:56
  227.2 0.0 copy-done
  227.2 3.7 %fusion.4 = f32[256,1024]{1,0:T(8,128)S(1)} fusion(f32[256,1024]{1,0:T(8,128)S(1)} %fusion.10, f32[1024,1024]{1,0:T(8,128)S(1)} %copy-done, s32[256]{0:T(256)S(1)} %iota_add_fusion), kind=kOutput, calls=%fused_computation.9 | convolution fusion | flops 3222274048 | bytes 6292480 | tf_op jit(solution)/shard_map/dot_general | solution.py:59
  231.0 0.0 copy-start.1
  231.0 4.7 %fusion.12 = f32[256,1024]{1,0:T(8,128)} fusion(f32[256,1024]{1,0:T(8,128)S(1)} %fusion.4, f32[1024,1024]{1,0:T(8,128)S(1)} %copy-done), kind=kOutput, calls=%fused_computation.25 | convolution fusion | flops 3221225472 | bytes 6291456 | tf_op jit(solution)/shard_map/dot_general | solution.py:63
  235.6 0.0 all-gather.5.cloned.1.call-update
  235.7 34.6 %all-gather.5.cloned.1.call-done = f32[1024,1024]{1,0:T(8,128)} async-done(((f32[256,1024]{1,0:T(8,128)}), f32[1024,1024]{1,0:T(8,128)}) %all-gather.5.cloned.1.call-update) | async-done | bytes 4194320 | tf_op jit(solution)/shard_map/all_gather | solution.py:69
  270.3 0.0 copy-done.1
  270.3 9.6 %divide_convert_fusion = bf16[512,1024]{1,0:T(8,128)(2,1)} fusion(f32[1024,1024]{1,0:T(8,128)} %all-gather.5.cloned.1.call-done, bf16[512,1024]{1,0:T(8,128)(2,1)S(1)} %copy-done.1, f32[]{:T(128)S(6)} %sqrt.7, f32[1024]{0:T(1024)S(1)} %get-tuple-element.14), kind=kOutput, calls=%fused_computation.2 | convolution fusion | flops 6444548096 | bytes 6295556 | tf_op jit(solution)/shard_map/dot_general | solution.py:67
  (4 shorter events, 0.0 us)
Async XLA Ops:
  6.5 82.8 %reduce-scatter.2.cloned.1.call-start = ((), (), s32[]{:S(2)}) async-start(), calls=%async_computation.1 | async-start | bytes 5242880 | tf_op jit(solution)/shard_map/reduce_scatter | solution.py:22
  48.4 122.7 %all-reduce.5.cloned.1.call-start = ((), (), s32[]{:S(2)}) async-start(), calls=%async_computation.2 | async-start | bytes 2097152 | tf_op jit(solution)/shard_map/psum | solution.py:40
  89.4 131.7 %all-gather.3.cloned.1.call-start = ((), (), s32[]{:S(2)}) async-start(), calls=%async_computation.3 | async-start | bytes 5242880 | tf_op jit(solution)/shard_map/all_gather | solution.py:55
  187.4 82.9 %all-gather.5.cloned.1.call-start = ((), (), s32[]{:S(2)}) async-start(), calls=%async_computation.4 | async-start | bytes 5242880 | tf_op jit(solution)/shard_map/all_gather | solution.py:69
  221.1 6.1 %copy-start = (f32[1024,1024]{1,0:T(8,128)S(1)}, f32[1024,1024]{1,0:T(8,128)}, u32[]{:S(2)}) copy-start(f32[1024,1024]{1,0:T(8,128)} %all-gather.3.cloned.1.call-done) | copy-start | bytes 12582916
  231.0 39.3 %copy-start.1 = (bf16[512,1024]{1,0:T(8,128)(2,1)S(1)}, bf16[512,1024]{1,0:T(8,128)(2,1)}, u32[]{:S(2)}) copy-start(bf16[512,1024]{1,0:T(8,128)(2,1)} %param.2) | copy-start | bytes 3145732
Sparse Core Ops, SparseCore 0:
  48.5 40.8 reduce-scatter.1
  92.9 78.1 all-reduce.4
  187.5 33.4 all-gather.2
  235.8 34.4 all-gather.4
